TPU v7x, 32 devices: a whole 2x2x4 slice. The times are simulated.
32 devices in a mesh: dp: 4 (over z), ctx: 8 (over y, x, core).
Axes of the slice: x: 2, y: 2, z: 4, core: 2. Of those that a mesh axis runs over, the one named last changes fastest.
Arguments:
- queries: bfloat16 [4, 1024, 2048], P('dp', 'ctx'), may hold values from -6 to 6
- keys: bfloat16 [4, 1024, 2048], P('dp', 'ctx'), may hold values from -6 to 6
- values: bfloat16 [4, 1024, 2048], P('dp', 'ctx'), may hold values from -6 to 6
- prior_state: float32 [4, 16, 128, 128], P('dp'), may hold values from -96 to 96
- norm_gain: float32 [2048], replicated, may hold values from 0.1 to 1.9
- router_weight: bfloat16 [2048, 32], replicated, may hold values from -0.125 to 0.125
- expert_ids: int32 [4, 1024, 4], P('dp', 'ctx'), may hold values from 0 to 31, all different within a row; in each aligned block of 128 rows (0 to 127, 128 to 255, ..., all dimensions but the last counted through in order) at most 24 rows name the same one
- w_gate: bfloat16 [32, 2048, 768], P(('dp', 'ctx')), may hold values from -0.125 to 0.125
- w_up: bfloat16 [32, 2048, 768], P(('dp', 'ctx')), may hold values from -0.125 to 0.125
- w_down: bfloat16 [32, 768, 2048], P(('dp', 'ctx')), may hold values from -0.21875 to 0.21875
- cotangent: bfloat16 [4, 1024, 2048], P('dp', 'ctx'), may hold values from -6 to 6
Outputs:
- output: bfloat16 [4, 1024, 2048], P('dp', 'ctx')
- grad_queries: bfloat16 [4, 1024, 2048], P('dp', 'ctx')
- grad_keys: bfloat16 [4, 1024, 2048], P('dp', 'ctx')
- grad_values: bfloat16 [4, 1024, 2048], P('dp', 'ctx')
- grad_gate: bfloat16 [32, 2048, 768], P(('dp', 'ctx'))
- grad_up: bfloat16 [32, 2048, 768], P(('dp', 'ctx'))
- grad_down: bfloat16 [32, 768, 2048], P(('dp', 'ctx'))
- grad_router: float32 [2048, 32], replicated
Inputs may be any that keep to these rules, and one draw needn't show every extreme that they name: `expert_ids`: within the rows of one device (aligned blocks of 128 tokens) no expert is named more than 24 times, and in every draw some expert is named exactly 24 times there; the 4 ids of one token differ.
All inputs are finite; a program needn't handle non-finite values.
Results may differ from a plain program's by a relative error of at most 0.012.
Values may be sent and summed in bfloat16 or wider, within the bound.
No kernel may reach another device: no remote copies, remote signals or barrier semaphores. Data moves between devices by JAX's collectives and lax.ppermute only.
A program may use at most 192 MiB of HBM per device.

v0:
```python
import jax
import jax.numpy as jnp
from jax import lax
from jax.sharding import PartitionSpec as P

H = 16
DH = 128
D = 2048
TOPK = 4
epsilon = 1e-05
exact_mode = lax.Precision.HIGHEST


def carried_in(value, axis, join, neutral):
    count, mine = (lax.axis_size(axis), lax.axis_index(axis))
    pieces = lax.all_gather(value, axis)
    total = jnp.full_like(value, 0) + jnp.asarray(neutral, value.dtype)

    def step(position, total):
        longer = join(total, pieces[position])
        return jnp.where(position < mine, longer, total)

    return lax.fori_loop(0, count - 1, step, total)


def entering(value, axis, join, neutral):
    count = lax.axis_size(axis)
    place = lax.axis_index(axis)
    ahead = count - 1 - place
    gathered = lax.all_gather(value.astype(jnp.bfloat16), axis)
    state = jnp.zeros_like(value) + jnp.asarray(neutral, value.dtype)

    def one(step, state):
        source = count - 1 - step
        return join(state, lax.dynamic_index_in_dim(gathered, source, 0, False).astype(value.dtype))

    return lax.fori_loop(0, ahead, one, state)


def add_states(earlier, later):
    return earlier + later


def expert_forward(inputs, gate_mat, up_mat, down_mat):
    gate_pre = jnp.dot(inputs, gate_mat, preferred_element_type=jnp.float32)
    up_pre = jnp.dot(inputs, up_mat, preferred_element_type=jnp.float32)
    gate_sig = jax.nn.sigmoid(gate_pre)
    hidden = (gate_pre * gate_sig * up_pre).astype(jnp.bfloat16)
    produced = jnp.dot(hidden, down_mat, preferred_element_type=jnp.float32).astype(jnp.bfloat16)
    return (gate_pre, up_pre, gate_sig, hidden, produced)


def expert_backward(
    inputs, grad_out, gate_pre, up_pre, gate_sig, hidden, gate_mat, up_mat, down_mat
):
    grad_hidden = jnp.dot(grad_out, down_mat.T, preferred_element_type=jnp.float32)
    grad_gate_pre = (grad_hidden * up_pre * gate_sig * (1.0 + gate_pre * (1.0 - gate_sig))).astype(
        jnp.bfloat16
    )
    grad_up_pre = (grad_hidden * gate_pre * gate_sig).astype(jnp.bfloat16)
    grad_down = jnp.dot(hidden.T, grad_out, preferred_element_type=jnp.float32).astype(jnp.bfloat16)
    grad_gate = jnp.dot(inputs.T, grad_gate_pre, preferred_element_type=jnp.float32).astype(
        jnp.bfloat16
    )
    grad_up = jnp.dot(inputs.T, grad_up_pre, preferred_element_type=jnp.float32).astype(
        jnp.bfloat16
    )
    grad_inputs = (
        jnp.dot(grad_gate_pre, gate_mat.T, preferred_element_type=jnp.float32)
        + jnp.dot(grad_up_pre, up_mat.T, preferred_element_type=jnp.float32)
    ).astype(jnp.bfloat16)
    return (grad_inputs, grad_gate, grad_up, grad_down)


def slot_layout(flat_ids, experts_all, capacity):
    count_assign = flat_ids.shape[0]
    onehot = (flat_ids[:, None] == jnp.arange(experts_all, dtype=jnp.int32)[None, :]).astype(
        jnp.int32
    )
    before = jnp.cumsum(onehot, axis=0) - onehot
    slot_rank = jnp.sum(before * onehot, axis=1)
    slot_index = flat_ids * capacity + slot_rank
    source = (
        jnp.full((experts_all * capacity,), -1, jnp.int32)
        .at[slot_index]
        .set(jnp.arange(count_assign, dtype=jnp.int32))
    )
    return (slot_index, source)


def route_rows(block):
    return lax.all_to_all(block, ("dp", "ctx"), split_axis=0, concat_axis=0, tiled=True)


def local(
    queries,
    keys,
    values,
    prior_state,
    norm_gain,
    router_weight,
    expert_ids,
    w_gate,
    w_up,
    w_down,
    cotangent,
):
    token_count = queries.shape[1]
    experts_all = router_weight.shape[1]
    capacity = max(2, 3 * token_count * TOPK // (2 * experts_all))
    queries3 = queries[0].reshape(token_count, H, DH)
    keys3 = keys[0].reshape(token_count, H, DH)
    values3 = values[0].reshape(token_count, H, DH)
    state_term = jnp.einsum("shi,shj->hij", keys3, values3, preferred_element_type=jnp.float32)
    zero_state = jnp.zeros_like(state_term)
    earlier_states = carried_in(state_term, "ctx", add_states, zero_state)
    state_in = prior_state[0] + earlier_states
    causal = jnp.arange(token_count)[:, None] >= jnp.arange(token_count)[None, :]
    scores = jnp.einsum("thd,shd->hts", queries3, keys3, preferred_element_type=jnp.float32)
    attn_scores = jnp.where(causal[None], scores, 0.0).astype(jnp.bfloat16)
    intra = jnp.einsum("hts,shj->thj", attn_scores, values3, preferred_element_type=jnp.float32)
    inter = jnp.einsum("thi,hij->thj", queries3.astype(jnp.float32), state_in, precision=exact_mode)
    attended = intra + inter
    gain_heads = norm_gain.reshape(H, DH)
    mean_square = jnp.mean(attended * attended, axis=-1, keepdims=True)
    scale_root = jnp.sqrt(mean_square + epsilon)
    mixed_rows = (attended / scale_root * gain_heads).astype(jnp.bfloat16).reshape(token_count, D)
    logits = jnp.dot(mixed_rows, router_weight, preferred_element_type=jnp.float32)
    token_ids = expert_ids[0]
    onehot_sel = (
        token_ids[:, :, None] == jnp.arange(experts_all, dtype=jnp.int32)[None, None, :]
    ).astype(jnp.float32)
    selected = jnp.sum(logits[:, None, :] * onehot_sel, axis=-1)
    gate_sig_r = jax.nn.sigmoid(selected)
    sig_total = jnp.sum(gate_sig_r, axis=1, keepdims=True)
    gates = gate_sig_r / sig_total
    slot_index, source = slot_layout(token_ids.reshape(-1), experts_all, capacity)
    filled = source >= 0
    row_of = jnp.where(filled, source // TOPK, 0)
    send_block = jnp.where(
        filled[:, None], mixed_rows[row_of], jnp.zeros((), jnp.bfloat16)
    ).reshape(experts_all, capacity, D)
    grad_y = cotangent[0].astype(jnp.float32)
    grad_out_assign = (
        (gates[:, :, None] * grad_y[:, None, :]).astype(jnp.bfloat16).reshape(token_count * TOPK, D)
    )
    send_grad = jnp.where(
        filled[:, None], grad_out_assign[jnp.where(filled, source, 0)], jnp.zeros((), jnp.bfloat16)
    ).reshape(experts_all, capacity, D)
    gate_mat = w_gate[0]
    up_mat = w_up[0]
    down_mat = w_down[0]
    received = route_rows(send_block).reshape(-1, D)
    gate_pre, up_pre, gate_sig, hidden, produced = expert_forward(
        received, gate_mat, up_mat, down_mat
    )
    returned = route_rows(produced.reshape(experts_all, capacity, D)).reshape(-1, D)
    received_grad = route_rows(send_grad).reshape(-1, D)
    grad_inputs, grad_gate, grad_up, grad_down = expert_backward(
        received, received_grad, gate_pre, up_pre, gate_sig, hidden, gate_mat, up_mat, down_mat
    )
    returned_grad = route_rows(grad_inputs.reshape(experts_all, capacity, D)).reshape(-1, D)
    out_float = returned[slot_index].reshape(token_count, TOPK, D).astype(jnp.float32)
    moe_sum = jnp.sum(gates[:, :, None] * out_float, axis=1)
    output = (mixed_rows.astype(jnp.float32) + moe_sum).astype(jnp.bfloat16)
    grad_gates = jnp.sum(out_float * grad_y[:, None, :], axis=-1)
    grad_assign = returned_grad[slot_index].reshape(token_count, TOPK, D).astype(jnp.float32)
    grad_moe = jnp.sum(gates[:, :, None] * grad_assign, axis=1)
    weighted_sum = jnp.sum(gates * grad_gates, axis=1, keepdims=True)
    grad_selected = gate_sig_r * (1.0 - gate_sig_r) * (grad_gates - weighted_sum) / sig_total
    grad_logits = jnp.sum(grad_selected[:, :, None] * onehot_sel, axis=1)
    router_term = jnp.dot(mixed_rows.astype(jnp.float32).T, grad_logits, precision=exact_mode)
    grad_router = lax.psum(router_term, ("dp", "ctx"))
    router_back = jnp.dot(grad_logits, router_weight.astype(jnp.float32).T, precision=exact_mode)
    grad_mixed = grad_y + grad_moe + router_back
    weighted = gain_heads * grad_mixed.reshape(token_count, H, DH)
    inner = jnp.sum(weighted * attended, axis=-1, keepdims=True)
    grad_attended = (
        (weighted - attended * (inner / (DH * (mean_square + epsilon)))) / scale_root
    ).astype(jnp.bfloat16)
    grad_term = jnp.einsum(
        "thi,thj->hij", queries3, grad_attended, preferred_element_type=jnp.float32
    )
    later_states = entering(grad_term, "ctx", add_states, zero_state)
    grad_scores = jnp.where(
        causal[None],
        jnp.einsum("thj,shj->hts", grad_attended, values3, preferred_element_type=jnp.float32),
        0.0,
    ).astype(jnp.bfloat16)
    grad_q = jnp.einsum(
        "hts,shi->thi", grad_scores, keys3, preferred_element_type=jnp.float32
    ) + jnp.einsum(
        "thj,hij->thi", grad_attended.astype(jnp.float32), state_in, precision=exact_mode
    )
    grad_k = jnp.einsum(
        "hts,thi->shi", grad_scores, queries3, preferred_element_type=jnp.float32
    ) + jnp.einsum("shj,hij->shi", values3.astype(jnp.float32), later_states, precision=exact_mode)
    grad_v = jnp.einsum(
        "hts,thj->shj", attn_scores, grad_attended, preferred_element_type=jnp.float32
    ) + jnp.einsum("shi,hij->shj", keys3.astype(jnp.float32), later_states, precision=exact_mode)
    row_shape = (1, token_count, D)
    return (
        output.reshape(row_shape),
        grad_q.astype(jnp.bfloat16).reshape(row_shape),
        grad_k.astype(jnp.bfloat16).reshape(row_shape),
        grad_v.astype(jnp.bfloat16).reshape(row_shape),
        grad_gate[None],
        grad_up[None],
        grad_down[None],
        grad_router,
    )


def solution(mesh):
    placed = (
        P("dp", "ctx", None),
        P("dp", "ctx", None),
        P("dp", "ctx", None),
        P("dp", None, None, None),
        P(),
        P(),
        P("dp", "ctx", None),
        P(("dp", "ctx"), None, None),
        P(("dp", "ctx"), None, None),
        P(("dp", "ctx"), None, None),
        P("dp", "ctx", None),
    )
    return jax.shard_map(
        local,
        mesh=mesh,
        in_specs=placed,
        out_specs=(
            P("dp", "ctx", None),
            P("dp", "ctx", None),
            P("dp", "ctx", None),
            P("dp", "ctx", None),
            P(("dp", "ctx"), None, None),
            P(("dp", "ctx"), None, None),
            P(("dp", "ctx"), None, None),
            P(),
        ),
        check_vma=False,
    )
```

profile of v0, /device:TPU:0, one launch (start us, length us, event | category | flops | bytes accessed | tf_op | source)
XLA Modules:
  0.0 655.8 jit_solution(7271364659372480334)
XLA Ops:
  20.3 3.1 mul.169
  23.4 5.5 mul.170
  33.3 2.5 fusion.17
  35.8 37.3 %all-gather.5.cloned.1.call-done = f32[128,128,128]{2,1,0:T(8,128)} async-done(((f32[16,128,128]{2,1,0:T(8,128)}), f32[128,128,128]{2,1,0:T(8,128)}) %all-gather.5.cloned.1.call-update) | async-done | bytes 8388624 | tf_op jit(solution)/shard_map/all_gather | solution.py:16
  73.1 18.7 %while.27 = (s32[]{:T(128)}, f32[16,128,128]{2,1,0:T(8,128)}, s32[]{:T(128)}, f32[8,16,128,128]{3,2,1,0:T(8,128)}, s32[]{:T(128)}, /*index=5*/s32[]{:T(128)}) while((s32[]{:T(128)}, f32[16,128,128]{2,1,0:T(8,128)}, s32[]{:T(128)}, f32[8,16,128,128]{3,2,1,0:T(8,128)}, s32[]{:T(128)}, /*index=5*/s32[]{:T(128)}) %tuple.85), condition=%wide.region_1.2_spmd.clone, body=%wide.region_0.1_spmd.clone.sunk | while | flops 786436 | bytes 3145821 | solution.py:23
  75.5 2.7 add_select_fusion.3
  78.2 2.7 add_select_fusion.3
  80.9 2.7 add_select_fusion.3
  83.7 2.7 add_select_fusion.3
  86.4 2.7 add_select_fusion.3
  89.1 2.7 add_select_fusion.3
  91.8 2.8 convolution_bitcast_fusion.5
  100.9 3.8 multiply_convert_fusion
  104.7 8.9 %gather_fusion.2 = bf16[768,2048]{1,0:T(8,128)(2,1)} fusion(bf16[512,2048]{1,0:T(8,128)(2,1)} %multiply_convert_fusion, s32[1024]{0:T(1024)S(1)} %get-tuple-element.236), kind=kCustom, calls=%fused_computation.2 | custom fusion | bytes 6294528 | tf_op jit(solution)/shard_map/gather | solution.py:148
  113.6 8.2 %gather_fusion = bf16[768,2048]{1,0:T(8,128)(2,1)} fusion(bf16[128,2048]{1,0:T(8,128)(2,1)} %copy.143, s32[1024]{0:T(1024)S(1)} %get-tuple-element.237), kind=kCustom, calls=%fused_computation | custom fusion | bytes 6294528 | tf_op jit(solution)/shard_map/gather | solution.py:141
  121.8 4.3 broadcast_select_fusion
  126.1 76.1 %all_to_all.20 = bf16[32,24,2048]{2,1,0:T(8,128)(2,1)} all-to-all(bf16[32,24,2048]{2,1,0:T(8,128)(2,1)S(1)} %get-tuple-element.231), channel_id=1, replica_groups=mesh['dp'=4,'ctx'=8] {'dp','ctx'}, dimensions={0} | all-to-all | bytes 6291456 | tf_op jit(solution)/shard_map/all_to_all | solution.py:92
  202.2 3.8 all-to-all-start.2
  206.0 7.0 %fusion.4 = f32[768,768]{1,0:T(8,128)} fusion(bf16[768,2048]{1,0:T(8,128)(2,1)} %bitcast.170, bf16[1,2048,768]{2,1,0:T(8,128)(2,1)} %param.23), kind=kOutput, calls=%fused_computation.20 | convolution fusion | flops 2415919104 | bytes 8650752 | tf_op jit(solution)/shard_map/dot_general | solution.py:46
  213.0 4.0 fusion.8
  217.1 60.4 %all-to-all-done.2 = bf16[32,24,2048]{2,1,0:T(8,128)(2,1)} async-done(((bf16[32,24,2048]{2,1,0:T(8,128)(2,1)}), bf16[32,24,2048]{2,1,0:T(8,128)(2,1)}, u32[]{:S(2)}, u32[]{:S(2)}) %all-to-all-start.2) | async-done | bytes 3145760 | tf_op jit(solution)/shard_map/all_to_all | solution.py:92
  277.5 7.9 %multiply_convert_fusion.1 = (bf16[768,768]{1,0:T(8,128)(2,1)S(1)}, bf16[768,768]{1,0:T(8,128)(2,1)S(1)}, bf16[768,768]{1,0:T(8,128)(2,1)}) fusion(f32[768,768]{1,0:T(8,128)} %fusion.8, f32[768,768]{1,0:T(8,128)} %fusion.4, bf16[768,2048]{1,0:T(8,128)(2,1)} %bitcast.23, bf16[1,768,2048]{2,1,0:T(8,128)(2,1)S(1)} %copy-done), kind=kOutput, calls=%fused_computation.32 | convolution fusion | flops 2425356288 | bytes 14548992 | tf_op jit(solution)/shard_map/dot_general | solution.py:56
  285.4 2.6 fusion.6
  288.1 4.0 add_convert_fusion
  292.1 4.0 all-to-all-start.3
  296.1 5.2 convolution_convert_fusion.3
  301.3 66.2 %all-to-all-done.3 = bf16[32,24,2048]{2,1,0:T(8,128)(2,1)} async-done(((bf16[32,24,2048]{2,1,0:T(8,128)(2,1)}), bf16[32,24,2048]{2,1,0:T(8,128)(2,1)}, u32[]{:S(2)}, u32[]{:S(2)}) %all-to-all-start.3) | async-done | bytes 3145760 | tf_op jit(solution)/shard_map/all_to_all | solution.py:92
  367.6 4.0 all-to-all-start.1
  371.9 7.5 %gather_fusion.3 = bf16[512,2048]{1,0:T(8,128)(2,1)} fusion(bf16[768,2048]{1,0:T(8,128)(2,1)} %bitcast.25, s32[1024]{0:T(1024)S(1)} %pad_clamp_fusion.1), kind=kCustom, calls=%fused_computation.3 | custom fusion | bytes 4196352 | tf_op jit(solution)/shard_map/gather | solution.py:167
  379.4 4.7 reshape.283
  384.1 59.0 %all-to-all-done.1 = bf16[32,24,2048]{2,1,0:T(8,128)(2,1)} async-done(((bf16[32,24,2048]{2,1,0:T(8,128)(2,1)}), bf16[32,24,2048]{2,1,0:T(8,128)(2,1)}, u32[]{:S(2)}, u32[]{:S(2)}) %all-to-all-start.1) | async-done | bytes 3145760 | tf_op jit(solution)/shard_map/all_to_all | solution.py:92
  443.1 7.5 %gather_fusion.1 = bf16[512,2048]{1,0:T(8,128)(2,1)} fusion(bf16[768,2048]{1,0:T(8,128)(2,1)} %bitcast.18, s32[1024]{0:T(1024)S(1)} %pad_clamp_fusion.1), kind=kCustom, calls=%fused_computation.1 | custom fusion | bytes 4196352 | tf_op jit(solution)/shard_map/gather | solution.py:163
  450.6 4.7 reshape.279
  455.4 11.2 %multiply_reduce_fusion = (f32[128,4]{1,0:T(8,128)S(1)}, f32[128,2048]{1,0:T(8,128)}, f32[128,2048]{1,0:T(8,128)}) fusion(f32[128,4,2048]{2,1,0:T(4,128)} %reshape.279, f32[128,2048]{1,0:T(8,128)} %copy-done.4, f32[128,4]{1,0:T(8,128)S(1)} %copy.138, f32[128,4,2048]{2,1,0:T(4,128)} %reshape.283), kind=kLoop, calls=%fused_computation.8 | loop fusion | flops 5766656 | bytes 11538432 | tf_op jit(solution)/shard_map/reduce_sum | solution.py:166
  466.7 3.0 convolution_add_fusion
  469.6 2.5 copy.148
  482.4 2.5 copy.144
  484.9 7.0 %fusion.10 = bf16[1,2048,768]{2,1,0:T(8,128)(2,1)} fusion(bf16[768,2048]{1,0:T(8,128)(2,1)} %bitcast.171, bf16[768,768]{1,0:T(8,128)(2,1)} %copy-done.26), kind=kOutput, calls=%fused_computation.28 | convolution fusion | flops 2417491968 | bytes 7471104 | tf_op jit(solution)/shard_map/dot_general | solution.py:62
  491.9 4.1 fusion.11
  496.0 6.1 fusion.12
  517.3 17.3 %while.26 = (s32[]{:T(128)}, f32[16,128,128]{2,1,0:T(8,128)}, s32[]{:T(128)}, bf16[8,16,128,128]{3,2,1,0:T(8,128)(2,1)}, s32[]{:T(128)}, /*index=5*/s32[]{:T(128)}, s32[]{:T(128)}, s32[]{:T(128)}) while((s32[]{:T(128)}, f32[16,128,128]{2,1,0:T(8,128)}, s32[]{:T(128)}, bf16[8,16,128,128]{3,2,1,0:T(8,128)(2,1)}, s32[]{:T(128)}, ...), condition=%wide.region_16.17_spmd, body=%wide.region_15.16_spmd.sunk | while | flops 524294 | bytes 2621575 | solution.py:37
  517.3 2.5 convert_add_fusion.2
  519.8 2.5 convert_add_fusion.2
  527.2 2.5 convert_add_fusion.2
  532.2 2.5 convert_add_fusion.2
  534.7 2.7 convolution_bitcast_fusion.3
  537.4 2.9 fusion.16
  545.5 101.8 %all-reduce.2.cloned.1.call-done = f32[2048,32]{0,1:T(8,128)} async-done(((f32[2048,32]{0,1:T(8,128)}), f32[2048,32]{0,1:T(8,128)}) %all-reduce.2.cloned.1.call-update) | async-done | bytes 262160 | tf_op jit(solution)/shard_map/psum | solution.py:173
  (131 shorter events, 66.1 us)
Async XLA Ops:
  7.2 270.3 %copy-start = (bf16[1,768,2048]{2,1,0:T(8,128)(2,1)S(1)}, bf16[1,768,2048]{2,1,0:T(8,128)(2,1)}, u32[]{:S(2)}) copy-start(bf16[1,768,2048]{2,1,0:T(8,128)(2,1)} %param.24) | copy-start | bytes 9437188
  7.2 65.9 %all-gather.5.cloned.1.call-start = ((), (), s32[]{:S(2)}) async-start(), calls=%async_computation.5 | async-start | bytes 9437184 | tf_op jit(solution)/shard_map/all_gather | solution.py:16
  7.2 8.7 %copy-start.22 = (s32[1,128,4]{1,2,0:T(4,128)S(1)}, s32[1,128,4]{1,2,0:T(4,128)}, u32[]{:S(2)}) copy-start(s32[1,128,4]{1,2,0:T(4,128)} %param.21) | copy-start | bytes 6148
  12.7 0.8 copy-start.9
  19.3 1.0 copy-start.4
  91.8 2.8 copy-start.10
  91.8 2.8 copy-start.19
  91.8 4.3 copy-start.21
  94.6 4.7 copy-start.20
  95.2 1.0 copy-start.3
  202.2 75.2 %all-to-all-start.2 = ((bf16[32,24,2048]{2,1,0:T(8,128)(2,1)}), bf16[32,24,2048]{2,1,0:T(8,128)(2,1)}, u32[]{:S(2)}, u32[]{:S(2)}) async-start(bf16[32,24,2048]{2,1,0:T(8,128)(2,1)} %get-tuple-element.230), calls=%async_computation.2 | async-start | bytes 6291456 | tf_op jit(solution)/shard_map/all_to_all | solution.py:92
  206.0 7.0 %copy-start.15 = (bf16[32,24,2048]{2,1,0:T(8,128)(2,1)S(1)}, bf16[32,24,2048]{2,1,0:T(8,128)(2,1)}, u32[]{:S(2)}) copy-start(bf16[32,24,2048]{2,1,0:T(8,128)(2,1)} %all_to_all.20) | copy-start | bytes 9437188
  206.0 7.0 %copy-start.23 = (bf16[1,2048,768]{2,1,0:T(8,128)(2,1)S(1)}, bf16[1,2048,768]{2,1,0:T(8,128)(2,1)}, u32[]{:S(2)}) copy-start(bf16[1,2048,768]{2,1,0:T(8,128)(2,1)} %param.22) | copy-start | bytes 9437188
  277.5 7.9 %copy-start.24 = (bf16[1,2048,768]{2,1,0:T(8,128)(2,1)S(1)}, bf16[1,2048,768]{2,1,0:T(8,128)(2,1)}, u32[]{:S(2)}) copy-start(bf16[1,2048,768]{2,1,0:T(8,128)(2,1)} %param.22) | copy-start | bytes 9437188
  285.3 2.7 copy-start.26
  285.3 2.7 copy-start.28
  285.3 2.7 copy-start.25
  292.1 75.5 %all-to-all-start.3 = ((bf16[32,24,2048]{2,1,0:T(8,128)(2,1)}), bf16[32,24,2048]{2,1,0:T(8,128)(2,1)}, u32[]{:S(2)}, u32[]{:S(2)}) async-start(bf16[32,24,2048]{2,1,0:T(8,128)(2,1)} %bitcast.175), calls=%async_computation.3 | async-start | bytes 6291456 | tf_op jit(solution)/shard_map/all_to_all | solution.py:92
  367.6 75.5 %all-to-all-start.1 = ((bf16[32,24,2048]{2,1,0:T(8,128)(2,1)}), bf16[32,24,2048]{2,1,0:T(8,128)(2,1)}, u32[]{:S(2)}, u32[]{:S(2)}) async-start(bf16[32,24,2048]{2,1,0:T(8,128)(2,1)} %bitcast.174), calls=%async_computation.1 | async-start | bytes 6291456 | tf_op jit(solution)/shard_map/all_to_all | solution.py:92
  371.6 144.6 %all-gather.7.cloned.1.call-start = ((), (), s32[]{:S(2)}) async-start(), calls=%async_computation.6 | async-start | bytes 4718592 | tf_op jit(solution)/shard_map/all_gather | solution.py:30
  472.2 4.7 copy-start.5
  476.0 0.8 copy-start.7
  480.0 167.3 %all-reduce.2.cloned.1.call-start = ((), (), s32[]{:S(2)}) async-start(), calls=%async_computation.4 | async-start | bytes 524288 | tf_op jit(solution)/shard_map/psum | solution.py:173
  484.9 7.0 %copy-start.16 = (bf16[32,24,2048]{2,1,0:T(8,128)(2,1)S(1)}, bf16[32,24,2048]{2,1,0:T(8,128)(2,1)}, u32[]{:S(2)}) copy-start(bf16[32,24,2048]{2,1,0:T(8,128)(2,1)} %all_to_all.20) | copy-start | bytes 9437188
  484.9 7.0 %copy-start.29 = (bf16[768,768]{1,0:T(8,128)(2,1)S(1)}, bf16[768,768]{1,0:T(8,128)(2,1)}, u32[]{:S(2)}) copy-start(bf16[768,768]{1,0:T(8,128)(2,1)} %copy-done.28) | copy-start | bytes 3538948
  491.9 4.1 copy-start.27
  496.0 6.1 copy-start.8
  496.0 6.1 copy-start.11
  496.0 6.6 %copy-start.2 = (f32[16,128,128]{2,1,0:T(8,128)S(1)}, f32[16,128,128]{2,1,0:T(8,128)}, u32[]{:S(2)}) copy-start(f32[16,128,128]{2,1,0:T(8,128)} %get-tuple-element.143) | copy-start | bytes 3145732
  496.0 6.6 %copy-start.13 = (f32[1,16,128,128]{3,2,1,0:T(8,128)S(1)}, f32[1,16,128,128]{3,2,1,0:T(8,128)}, u32[]{:S(2)}) copy-start(f32[1,16,128,128]{3,2,1,0:T(8,128)} %param.18) | copy-start | bytes 3145732
  502.1 1.2 copy-start.12
  502.6 2.0 copy-start.17
  534.7 2.7 copy-start.1
  534.7 2.8 copy-start.14
  534.7 5.6 copy-start.6
  534.7 5.6 copy-start.18
Sparse Core Ops, SparseCore 0:
  16.0 57.0 all-gather.4
  480.1 36.0 all-gather.6
  522.3 124.9 all-reduce.1
where the time goes:
time: 666 us; the launch traced here: 656 us
  waiting for transfers between devices  327 us (49%)
  local copies, waits for them, and re-layouts  83.1 us (12%)
  blocking collectives  76.1 us (11%)
  matrix products  75.4 us (11%)
  other arithmetic  67.4 us (10%)
  between operations  14.4 us (2%)
  starting transfers between devices  12.4 us (2%)
    all_to_all x3, waiting for transfers between devices, route_rows(): lax.all_to_all(block, ('dp', 'ctx'), split_axis=0, concat_axis=0, tiled=T...  186 us
    psum x1, waiting for transfers between devices, local(): grad_router = lax.psum(router_term, ('dp', 'ctx'))  102 us
    all_to_all x1, blocking collectives, route_rows(): lax.all_to_all(block, ('dp', 'ctx'), split_axis=0, concat_axis=0, tiled=T...  76.1 us
    all_gather x1, waiting for transfers between devices, carried_in(): pieces = lax.all_gather(value, axis)  37.3 us
    select_n x7, other arithmetic, step(): return jnp.where(position < mine, longer, total)  18.7 us
    add x7, other arithmetic, add_states(): return earlier + later  17.3 us
    unnamed x68, local copies, waits for them, and re-layouts  16.8 us
  transfers between devices with their start and end apart: 6, of which 6 were waited for; matrix products, arithmetic and copies ran while one was open for 17% of the time, Pallas kernels for 0%

commit v1 on v0

--- a/solution.py
+++ b/solution.py
@@ -170,7 +170,8 @@
     grad_selected = gate_sig_r * (1.0 - gate_sig_r) * (grad_gates - weighted_sum) / sig_total
     grad_logits = jnp.sum(grad_selected[:, :, None] * onehot_sel, axis=1)
     router_term = jnp.dot(mixed_rows.astype(jnp.float32).T, grad_logits, precision=exact_mode)
-    grad_router = lax.psum(router_term, ("dp", "ctx"))
+    half = lax.psum(router_term, "ctx")
+    grad_router = lax.psum(half, "dp")
     router_back = jnp.dot(grad_logits, router_weight.astype(jnp.float32).T, precision=exact_mode)
     grad_mixed = grad_y + grad_moe + router_back
     weighted = gain_heads * grad_mixed.reshape(token_count, H, DH)

time: 666 us -> 627 us (0.941)
  waiting for transfers between devices: 327 us -> 284 us
    psum x1 -> x2, waiting for transfers between devices: 102 us -> 23.2 us  [the longest x1 17.4 us: local(): half = lax.psum(router_term, 'ctx')]
    all_gather x1, waiting for transfers between devices: 2.22 us -> 38.2 us  [entering(): gathered = lax.all_gather(value.astype(jnp.bfloat16), axis)]
    unnamed x68 -> x60, local copies, waits for them, and re-layouts: 16.8 us -> 16 us
  transfers between devices with their start and end apart: 6 -> 7, of which waited for: 6 -> 7; matrix products, arithmetic and copies ran while one was open for 17% -> 19% of each run, Pallas kernels for 0% -> 0%
where the time goes in v1:
time: 627 us; the launch traced here: 616 us
  waiting for transfers between devices  284 us (45%)
  local copies, waits for them, and re-layouts  82.3 us (13%)
  matrix products  78.7 us (13%)
  blocking collectives  76.1 us (12%)
  other arithmetic  68.1 us (11%)
  between operations  14.4 us (2%)
  starting transfers between devices  12.4 us (2%)
    all_to_all x3, waiting for transfers between devices, route_rows(): lax.all_to_all(block, ('dp', 'ctx'), split_axis=0, concat_axis=0, tiled=T...  186 us
    all_to_all x1, blocking collectives, route_rows(): lax.all_to_all(block, ('dp', 'ctx'), split_axis=0, concat_axis=0, tiled=T...  76.1 us
    all_gather x1, waiting for transfers between devices, entering(): gathered = lax.all_gather(value.astype(jnp.bfloat16), axis)  38.2 us
    all_gather x1, waiting for transfers between devices, carried_in(): pieces = lax.all_gather(value, axis)  37.3 us
    select_n x7, other arithmetic, step(): return jnp.where(position < mine, longer, total)  18.6 us
    psum x1, waiting for transfers between devices, local(): half = lax.psum(router_term, 'ctx')  17.4 us
    add x7, other arithmetic, add_states(): return earlier + later  17.3 us
    unnamed x60, local copies, waits for them, and re-layouts  16 us
  transfers between devices with their start and end apart: 7, of which 7 were waited for; matrix products, arithmetic and copies ran while one was open for 19% of the time, Pallas kernels for 0%

profile of v1, /device:TPU:0, one launch (start us, length us, event | category | flops | bytes accessed | tf_op | source)
XLA Modules:
  0.0 616.3 jit_solution(11355157116386442579)
XLA Ops:
  20.3 3.1 mul.169
  23.4 5.5 mul.170
  33.3 2.5 fusion.17
  35.8 37.3 %all-gather.5.cloned.1.call-done = f32[128,128,128]{2,1,0:T(8,128)} async-done(((f32[16,128,128]{2,1,0:T(8,128)}), f32[128,128,128]{2,1,0:T(8,128)}) %all-gather.5.cloned.1.call-update) | async-done | bytes 8388624 | tf_op jit(solution)/shard_map/all_gather | solution.py:16
  73.1 18.6 %while.27 = (s32[]{:T(128)}, f32[16,128,128]{2,1,0:T(8,128)}, s32[]{:T(128)}, f32[8,16,128,128]{3,2,1,0:T(8,128)}, s32[]{:T(128)}, /*index=5*/s32[]{:T(128)}) while((s32[]{:T(128)}, f32[16,128,128]{2,1,0:T(8,128)}, s32[]{:T(128)}, f32[8,16,128,128]{3,2,1,0:T(8,128)}, s32[]{:T(128)}, /*index=5*/s32[]{:T(128)}) %tuple.87), condition=%wide.region_1.2_spmd.clone, body=%wide.region_0.1_spmd.clone.sunk | while | flops 786436 | bytes 3145821 | solution.py:23
  75.5 2.7 add_select_fusion.3
  78.2 2.7 add_select_fusion.3
  80.9 2.7 add_select_fusion.3
  83.6 2.7 add_select_fusion.3
  86.3 2.7 add_select_fusion.3
  89.0 2.7 add_select_fusion.3
  91.7 2.8 convolution_bitcast_fusion.5
  100.8 3.8 multiply_convert_fusion
  104.6 8.9 %gather_fusion.2 = bf16[768,2048]{1,0:T(8,128)(2,1)} fusion(bf16[512,2048]{1,0:T(8,128)(2,1)} %multiply_convert_fusion, s32[1024]{0:T(1024)S(1)} %get-tuple-element.236), kind=kCustom, calls=%fused_computation.2 | custom fusion | bytes 6294528 | tf_op jit(solution)/shard_map/gather | solution.py:148
  113.5 8.2 %gather_fusion = bf16[768,2048]{1,0:T(8,128)(2,1)} fusion(bf16[128,2048]{1,0:T(8,128)(2,1)} %copy.143, s32[1024]{0:T(1024)S(1)} %get-tuple-element.237), kind=kCustom, calls=%fused_computation | custom fusion | bytes 6294528 | tf_op jit(solution)/shard_map/gather | solution.py:141
  121.7 4.3 broadcast_select_fusion
  126.0 76.1 %all_to_all.20 = bf16[32,24,2048]{2,1,0:T(8,128)(2,1)} all-to-all(bf16[32,24,2048]{2,1,0:T(8,128)(2,1)S(1)} %get-tuple-element.231), channel_id=1, replica_groups=mesh['dp'=4,'ctx'=8] {'dp','ctx'}, dimensions={0} | all-to-all | bytes 6291456 | tf_op jit(solution)/shard_map/all_to_all | solution.py:92
  202.1 3.8 all-to-all-start.2
  205.9 7.0 %fusion.4 = f32[768,768]{1,0:T(8,128)} fusion(bf16[768,2048]{1,0:T(8,128)(2,1)} %bitcast.170, bf16[1,2048,768]{2,1,0:T(8,128)(2,1)} %param.23), kind=kOutput, calls=%fused_computation.20 | convolution fusion | flops 2415919104 | bytes 8650752 | tf_op jit(solution)/shard_map/dot_general | solution.py:46
  212.9 4.0 fusion.8
  216.9 60.4 %all-to-all-done.2 = bf16[32,24,2048]{2,1,0:T(8,128)(2,1)} async-done(((bf16[32,24,2048]{2,1,0:T(8,128)(2,1)}), bf16[32,24,2048]{2,1,0:T(8,128)(2,1)}, u32[]{:S(2)}, u32[]{:S(2)}) %all-to-all-start.2) | async-done | bytes 3145760 | tf_op jit(solution)/shard_map/all_to_all | solution.py:92
  277.3 7.9 %multiply_convert_fusion.1 = (bf16[768,768]{1,0:T(8,128)(2,1)S(1)}, bf16[768,768]{1,0:T(8,128)(2,1)S(1)}, bf16[768,768]{1,0:T(8,128)(2,1)}) fusion(f32[768,768]{1,0:T(8,128)} %fusion.8, f32[768,768]{1,0:T(8,128)} %fusion.4, bf16[768,2048]{1,0:T(8,128)(2,1)} %bitcast.23, bf16[1,768,2048]{2,1,0:T(8,128)(2,1)S(1)} %copy-done), kind=kOutput, calls=%fused_computation.32 | convolution fusion | flops 2425356288 | bytes 14548992 | tf_op jit(solution)/shard_map/dot_general | solution.py:56
  285.2 2.6 fusion.6
  288.0 4.0 add_convert_fusion
  291.9 4.0 all-to-all-start.3
  296.0 5.2 convolution_convert_fusion.3
  301.2 66.2 %all-to-all-done.3 = bf16[32,24,2048]{2,1,0:T(8,128)(2,1)} async-done(((bf16[32,24,2048]{2,1,0:T(8,128)(2,1)}), bf16[32,24,2048]{2,1,0:T(8,128)(2,1)}, u32[]{:S(2)}, u32[]{:S(2)}) %all-to-all-start.3) | async-done | bytes 3145760 | tf_op jit(solution)/shard_map/all_to_all | solution.py:92
  367.4 4.0 all-to-all-start.1
  371.7 7.5 %gather_fusion.3 = bf16[512,2048]{1,0:T(8,128)(2,1)} fusion(bf16[768,2048]{1,0:T(8,128)(2,1)} %bitcast.25, s32[1024]{0:T(1024)S(1)} %pad_clamp_fusion.1), kind=kCustom, calls=%fused_computation.3 | custom fusion | bytes 4196352 | tf_op jit(solution)/shard_map/gather | solution.py:167
  379.2 4.7 reshape.283
  384.0 59.0 %all-to-all-done.1 = bf16[32,24,2048]{2,1,0:T(8,128)(2,1)} async-done(((bf16[32,24,2048]{2,1,0:T(8,128)(2,1)}), bf16[32,24,2048]{2,1,0:T(8,128)(2,1)}, u32[]{:S(2)}, u32[]{:S(2)}) %all-to-all-start.1) | async-done | bytes 3145760 | tf_op jit(solution)/shard_map/all_to_all | solution.py:92
  442.9 7.5 %gather_fusion.1 = bf16[512,2048]{1,0:T(8,128)(2,1)} fusion(bf16[768,2048]{1,0:T(8,128)(2,1)} %bitcast.18, s32[1024]{0:T(1024)S(1)} %pad_clamp_fusion.1), kind=kCustom, calls=%fused_computation.1 | custom fusion | bytes 4196352 | tf_op jit(solution)/shard_map/gather | solution.py:163
  450.5 4.8 reshape.279
  455.2 11.2 %multiply_reduce_fusion = (f32[128,4]{1,0:T(8,128)S(1)}, f32[128,2048]{1,0:T(8,128)}, f32[128,2048]{1,0:T(8,128)}) fusion(f32[128,4,2048]{2,1,0:T(4,128)} %reshape.279, f32[128,2048]{1,0:T(8,128)} %copy-done.4, f32[128,4]{1,0:T(8,128)S(1)} %copy.138, f32[128,4,2048]{2,1,0:T(4,128)} %reshape.283), kind=kLoop, calls=%fused_computation.8 | loop fusion | flops 5766656 | bytes 11538432 | tf_op jit(solution)/shard_map/reduce_sum | solution.py:166
  468.9 3.0 convolution_add_fusion
  471.9 2.5 copy.148
  476.3 2.7 divide_convert_fusion
  485.8 2.5 copy.144
  488.3 6.7 %fusion.10 = bf16[1,2048,768]{2,1,0:T(8,128)(2,1)} fusion(bf16[768,2048]{1,0:T(8,128)(2,1)} %bitcast.171, bf16[768,768]{1,0:T(8,128)(2,1)} %copy-done.22), kind=kOutput, calls=%fused_computation.28 | convolution fusion | flops 2417491968 | bytes 7471104 | tf_op jit(solution)/shard_map/dot_general | solution.py:62
  495.1 4.1 fusion.11
  499.1 6.1 fusion.12
  514.7 17.4 %all-reduce.3.cloned.1.call-done = f32[2048,32]{0,1:T(8,128)} async-done(((f32[2048,32]{0,1:T(8,128)}), f32[2048,32]{0,1:T(8,128)}) %all-reduce.3.cloned.1.call-update) | async-done | bytes 262160 | tf_op jit(solution)/shard_map/psum | solution.py:173
  532.1 38.2 %all-gather.7.cloned.1.call-done = bf16[128,128,128]{2,1,0:T(8,128)(2,1)} async-done(((bf16[16,128,128]{2,1,0:T(8,128)(2,1)}), bf16[128,128,128]{2,1,0:T(8,128)(2,1)}) %all-gather.7.cloned.1.call-update) | async-done | bytes 4194320 | tf_op jit(solution)/shard_map/all_gather | solution.py:30
  571.4 17.3 %while.26 = (s32[]{:T(128)}, f32[16,128,128]{2,1,0:T(8,128)}, s32[]{:T(128)}, bf16[8,16,128,128]{3,2,1,0:T(8,128)(2,1)}, s32[]{:T(128)}, /*index=5*/s32[]{:T(128)}, s32[]{:T(128)}, s32[]{:T(128)}) while((s32[]{:T(128)}, f32[16,128,128]{2,1,0:T(8,128)}, s32[]{:T(128)}, bf16[8,16,128,128]{3,2,1,0:T(8,128)(2,1)}, s32[]{:T(128)}, ...), condition=%wide.region_16.17_spmd, body=%wide.region_15.16_spmd.sunk | while | flops 524294 | bytes 2621575 | solution.py:37
  588.7 3.7 convolution_bitcast_fusion.3
  592.4 2.9 fusion.16
  597.3 2.7 fusion.20
  602.1 5.8 all-reduce.5.cloned.1.call-done
  (126 shorter events, 71.1 us)
Async XLA Ops:
  7.2 270.2 %copy-start = (bf16[1,768,2048]{2,1,0:T(8,128)(2,1)S(1)}, bf16[1,768,2048]{2,1,0:T(8,128)(2,1)}, u32[]{:S(2)}) copy-start(bf16[1,768,2048]{2,1,0:T(8,128)(2,1)} %param.24) | copy-start | bytes 9437188
  7.2 65.9 %all-gather.5.cloned.1.call-start = ((), (), s32[]{:S(2)}) async-start(), calls=%async_computation.6 | async-start | bytes 9437184 | tf_op jit(solution)/shard_map/all_gather | solution.py:16
  7.2 8.7 %copy-start.18 = (s32[1,128,4]{1,2,0:T(4,128)S(1)}, s32[1,128,4]{1,2,0:T(4,128)}, u32[]{:S(2)}) copy-start(s32[1,128,4]{1,2,0:T(4,128)} %param.21) | copy-start | bytes 6148
  12.7 0.8 copy-start.6
  19.3 1.0 copy-start.4
  91.7 2.8 copy-start.7
  91.7 2.8 copy-start.15
  91.7 4.3 copy-start.17
  94.5 4.7 copy-start.16
  95.1 1.0 copy-start.3
  202.1 75.2 %all-to-all-start.2 = ((bf16[32,24,2048]{2,1,0:T(8,128)(2,1)}), bf16[32,24,2048]{2,1,0:T(8,128)(2,1)}, u32[]{:S(2)}, u32[]{:S(2)}) async-start(bf16[32,24,2048]{2,1,0:T(8,128)(2,1)} %get-tuple-element.230), calls=%async_computation.2 | async-start | bytes 6291456 | tf_op jit(solution)/shard_map/all_to_all | solution.py:92
  205.9 7.0 %copy-start.12 = (bf16[32,24,2048]{2,1,0:T(8,128)(2,1)S(1)}, bf16[32,24,2048]{2,1,0:T(8,128)(2,1)}, u32[]{:S(2)}) copy-start(bf16[32,24,2048]{2,1,0:T(8,128)(2,1)} %all_to_all.20) | copy-start | bytes 9437188
  205.9 7.0 %copy-start.19 = (bf16[1,2048,768]{2,1,0:T(8,128)(2,1)S(1)}, bf16[1,2048,768]{2,1,0:T(8,128)(2,1)}, u32[]{:S(2)}) copy-start(bf16[1,2048,768]{2,1,0:T(8,128)(2,1)} %param.22) | copy-start | bytes 9437188
  277.3 7.9 %copy-start.20 = (bf16[1,2048,768]{2,1,0:T(8,128)(2,1)S(1)}, bf16[1,2048,768]{2,1,0:T(8,128)(2,1)}, u32[]{:S(2)}) copy-start(bf16[1,2048,768]{2,1,0:T(8,128)(2,1)} %param.22) | copy-start | bytes 9437188
  285.2 2.7 copy-start.22
  285.2 2.7 copy-start.24
  285.2 2.7 copy-start.21
  291.9 75.5 %all-to-all-start.3 = ((bf16[32,24,2048]{2,1,0:T(8,128)(2,1)}), bf16[32,24,2048]{2,1,0:T(8,128)(2,1)}, u32[]{:S(2)}, u32[]{:S(2)}) async-start(bf16[32,24,2048]{2,1,0:T(8,128)(2,1)} %bitcast.175), calls=%async_computation.3 | async-start | bytes 6291456 | tf_op jit(solution)/shard_map/all_to_all | solution.py:92
  367.4 75.5 %all-to-all-start.1 = ((bf16[32,24,2048]{2,1,0:T(8,128)(2,1)}), bf16[32,24,2048]{2,1,0:T(8,128)(2,1)}, u32[]{:S(2)}, u32[]{:S(2)}) async-start(bf16[32,24,2048]{2,1,0:T(8,128)(2,1)} %bitcast.174), calls=%async_computation.1 | async-start | bytes 6291456 | tf_op jit(solution)/shard_map/all_to_all | solution.py:92
  371.5 160.6 %all-reduce.3.cloned.1.call-start = ((), (), s32[]{:S(2)}) async-start(), calls=%async_computation.4 | async-start | bytes 524288 | tf_op jit(solution)/shard_map/psum | solution.py:173
  479.0 91.2 %all-gather.7.cloned.1.call-start = ((), (), s32[]{:S(2)}) async-start(), calls=%async_computation.7 | async-start | bytes 4718592 | tf_op jit(solution)/shard_map/all_gather | solution.py:30
  483.5 124.4 %all-reduce.5.cloned.1.call-start = ((), (), s32[]{:S(2)}) async-start(), calls=%async_computation.5 | async-start | bytes 524288 | tf_op jit(solution)/shard_map/psum | solution.py:174
  488.3 6.7 %copy-start.13 = (bf16[32,24,2048]{2,1,0:T(8,128)(2,1)S(1)}, bf16[32,24,2048]{2,1,0:T(8,128)(2,1)}, u32[]{:S(2)}) copy-start(bf16[32,24,2048]{2,1,0:T(8,128)(2,1)} %all_to_all.20) | copy-start | bytes 9437188
  488.3 6.7 %copy-start.25 = (bf16[768,768]{1,0:T(8,128)(2,1)S(1)}, bf16[768,768]{1,0:T(8,128)(2,1)}, u32[]{:S(2)}) copy-start(bf16[768,768]{1,0:T(8,128)(2,1)} %copy-done.24) | copy-start | bytes 3538948
  495.0 4.1 copy-start.23
  499.1 6.1 copy-start.5
  499.1 6.1 copy-start.8
  499.1 6.6 %copy-start.2 = (f32[16,128,128]{2,1,0:T(8,128)S(1)}, f32[16,128,128]{2,1,0:T(8,128)}, u32[]{:S(2)}) copy-start(f32[16,128,128]{2,1,0:T(8,128)} %get-tuple-element.143) | copy-start | bytes 3145732
  499.1 6.6 %copy-start.10 = (f32[1,16,128,128]{3,2,1,0:T(8,128)S(1)}, f32[1,16,128,128]{3,2,1,0:T(8,128)}, u32[]{:S(2)}) copy-start(f32[1,16,128,128]{3,2,1,0:T(8,128)} %param.18) | copy-start | bytes 3145732
  505.2 1.2 copy-start.9
  505.8 2.0 copy-start.14
  588.7 3.7 copy-start.1
  588.7 3.7 copy-start.11
Sparse Core Ops, SparseCore 0:
  16.0 57.0 all-gather.4
  479.2 52.8 all-reduce.2
  534.1 36.0 all-gather.6
  572.5 35.2 all-reduce.4
